TPU v7x, 512 devices: a whole 4x4x16 slice. The times are simulated.
512 devices in a mesh: row: 16 (over x, y), col: 32 (over z, core).
Axes of the slice: x: 4, y: 4, z: 16, core: 2. Of those that a mesh axis runs over, the one named last changes fastest.
Arguments:
- front: bfloat16 [16384, 16384], P('row', 'col'), may hold values from -0.046875 to 0.046875
- diag_inverse: float32 [128, 128, 128], P('row'), may hold values from -0.25 to 1.5
- load: float32 [8, 16384], P(None, 'row'), may hold values from -6 to 6
- panel_order: int32 [128], replicated, may hold values from 0 to 127, each once
- tie: float32 [32, 16384], P('col', 'row'), may hold values from 0.5 to 1.5
- mass: float32 [32, 16384], P('col', 'row'), may hold values from 0.5 to 6
- modes: bfloat16 [1024, 32, 16384], P(None, 'col', 'row'), may hold values from -0.0234375 to 0.0234375
Outputs:
- front_solution: float32 [8, 16384], P(None, 'row')
- residual_vectors: float32 [8, 32, 16384], P(None, 'col', 'row')
All inputs are finite; a program needn't handle non-finite values.
Results may differ from a plain program's by a relative error of at most 0.0049.
Values may be sent and summed in bfloat16 or wider, within the bound.
No kernel may reach another device: no remote copies, remote signals or barrier semaphores. Data moves between devices by JAX's collectives and lax.ppermute only.
A program may use at most 64 MiB of HBM per device.

v0:
```python
import jax
import jax.numpy as jnp
from jax import lax
from jax.sharding import PartitionSpec as P

LEVELS = 4
highest = lax.Precision.HIGHEST


def on_device(front, diag_inverse, load, panel_order, tie, mass, modes):
    vectors = load.shape[0]
    block_size = diag_inverse.shape[1]
    local_panels = diag_inverse.shape[0]
    rows_local = front.shape[0]
    cols_local = front.shape[1]
    panels = panel_order.shape[0]
    row_at = lax.axis_index("row")
    col_at = lax.axis_index("col")
    counting = jnp.arange(panels, dtype=jnp.int32)
    matches = panel_order[:, None] == counting[None, :]
    ranks = jnp.sum(jnp.where(matches, counting[:, None], 0), axis=0)
    levels_of = ranks // (panels // LEVELS)
    position_level = jnp.repeat(levels_of, block_size)
    row_level = lax.dynamic_slice_in_dim(position_level, row_at * rows_local, rows_local, 0)
    pending = jnp.zeros((vectors, rows_local), jnp.float32)
    forward_out = jnp.zeros((vectors, rows_local), jnp.float32)
    for level in range(LEVELS):
        if level > 0:
            total_sum = lax.psum(pending, "col")
        else:
            total_sum = pending
        remain = (load - total_sum).reshape(vectors, local_panels, block_size)
        candidate = jnp.einsum("vpj,pij->vpi", remain, diag_inverse, precision=highest).reshape(
            vectors, rows_local
        )
        chosen = row_level[None, :] == level
        forward_out = jnp.where(chosen, candidate, forward_out)
        if level < LEVELS - 1:
            fresh = jnp.where(chosen, forward_out, 0.0).astype(jnp.bfloat16)
            whole = lax.all_gather(fresh, "row", axis=1, tiled=True)
            mine = lax.dynamic_slice_in_dim(whole, col_at * cols_local, cols_local, 1)
            pending = pending + jnp.dot(mine, front.T, preferred_element_type=jnp.float32)
    back_pending = jnp.zeros((vectors, cols_local), jnp.float32)
    back_out = jnp.zeros((vectors, rows_local), jnp.float32)
    for level in reversed(range(LEVELS)):
        if level < LEVELS - 1:
            column_sum = lax.psum(back_pending, "row")
            full_sum = lax.all_gather(column_sum, "col", axis=1, tiled=True)
            here = lax.dynamic_slice_in_dim(full_sum, row_at * rows_local, rows_local, 1)
        else:
            here = jnp.zeros((vectors, rows_local), jnp.float32)
        remain = (forward_out - here).reshape(vectors, local_panels, block_size)
        candidate = jnp.einsum("vpj,pji->vpi", remain, diag_inverse, precision=highest).reshape(
            vectors, rows_local
        )
        chosen = row_level[None, :] == level
        back_out = jnp.where(chosen, candidate, back_out)
        if level > 0:
            fresh = jnp.where(chosen, back_out, 0.0).astype(jnp.bfloat16)
            back_pending = back_pending + jnp.dot(fresh, front, preferred_element_type=jnp.float32)
    static = tie[None, :, :] * back_out[:, None, :]
    weighted = (mass[None, :, :] * static).astype(jnp.bfloat16).reshape(vectors, -1)
    mode_rows = modes.reshape(modes.shape[0], -1)
    partial_coords = lax.dot_general(
        weighted, mode_rows, (((1,), (1,)), ((), ())), preferred_element_type=jnp.float32
    )
    coords = lax.psum(partial_coords, ("row", "col"))
    correction = jnp.dot(coords.astype(jnp.bfloat16), mode_rows, preferred_element_type=jnp.float32)
    return (back_out, static - correction.reshape(static.shape))


def solution(mesh):
    in_specs = (
        P("row", "col"),
        P("row", None, None),
        P(None, "row"),
        P(),
        P("col", "row"),
        P("col", "row"),
        P(None, "col", "row"),
    )
    out_specs = (P(None, "row"), P(None, "col", "row"))
    return jax.shard_map(
        on_device, mesh=mesh, in_specs=in_specs, out_specs=out_specs, check_vma=False
    )
```

profile of v0, /device:TPU:1, one launch (start us, length us, event | category | flops | bytes accessed | tf_op | source)
XLA Modules:
  0.0 765.4 jit_solution(5559178636949547583)
XLA Ops:
  0.6 0.0 copy-start
  0.6 0.0 copy-start.1
  0.7 0.0 copy-start.2
  0.7 0.9 select_reduce_fusion
  1.6 0.1 broadcast_bitcast_fusion
  1.7 2.0 select_convert_fusion.5
  3.7 19.7 %all_gather.18 = bf16[8,16384]{1,0:T(8,128)(2,1)S(1)} all-gather(bf16[8,1024]{1,0:T(8,128)(2,1)S(1)} %get-tuple-element.14), channel_id=1, replica_groups=mesh['row'=16,'col'=32] {'row'}, dimensions={1}, use_global_device_ids=true | all-gather | bytes 278528 | tf_op jit(solution)/shard_map/all_gather | solution.py:40
  23.3 1.6 fusion.64
  24.9 99.0 %psum.49 = f32[8,1024]{1,0:T(8,128)S(1)} all-reduce(f32[8,1024]{1,0:T(8,128)S(1)} %fusion.64), channel_id=1, replica_groups=mesh['row'=16,'col'=32] {'col'}, use_global_device_ids=true, to_apply=%region_1.2 | all-reduce | flops 8192 | bytes 65536 | tf_op jit(solution)/shard_map/psum | solution.py:29
  123.9 0.0 copy-done.2
  123.9 2.0 select_convert_fusion.4
  125.9 17.9 %all_gather.19 = bf16[8,16384]{1,0:T(8,128)(2,1)S(1)} all-gather(bf16[8,1024]{1,0:T(8,128)(2,1)S(1)} %get-tuple-element.8), channel_id=1, replica_groups=mesh['row'=16,'col'=32] {'row'}, dimensions={1}, use_global_device_ids=true | all-gather | bytes 278528 | tf_op jit(solution)/shard_map/all_gather | solution.py:40
  143.8 0.0 copy-done.1
  143.8 0.4 convolution_add_fusion.1
  144.2 95.2 %psum.50 = f32[8,1024]{1,0:T(8,128)S(1)} all-reduce(f32[8,1024]{1,0:T(8,128)S(1)} %convolution_add_fusion.1), channel_id=1, replica_groups=mesh['row'=16,'col'=32] {'col'}, use_global_device_ids=true, to_apply=%region_2.3 | all-reduce | flops 8192 | bytes 65536 | tf_op jit(solution)/shard_map/psum | solution.py:29
  239.4 2.0 select_convert_fusion.3
  241.4 16.6 %all_gather.20 = bf16[8,16384]{1,0:T(8,128)(2,1)S(1)} all-gather(bf16[8,1024]{1,0:T(8,128)(2,1)S(1)} %get-tuple-element.17), channel_id=1, replica_groups=mesh['row'=16,'col'=32] {'row'}, dimensions={1}, use_global_device_ids=true | all-gather | bytes 278528 | tf_op jit(solution)/shard_map/all_gather | solution.py:40
  258.0 0.4 convolution_add_fusion
  258.4 94.9 %psum.51 = f32[8,1024]{1,0:T(8,128)S(1)} all-reduce(f32[8,1024]{1,0:T(8,128)S(1)} %convolution_add_fusion), channel_id=1, replica_groups=mesh['row'=16,'col'=32] {'col'}, use_global_device_ids=true, to_apply=%region_3.4 | all-reduce | flops 8192 | bytes 65536 | tf_op jit(solution)/shard_map/psum | solution.py:29
  353.3 2.0 bitcast_select_fusion.5
  355.3 1.6 fusion.22
  356.9 0.2 fusion.40
  357.1 58.2 %psum.52 = f32[8,512]{1,0:T(8,128)S(1)} all-reduce(f32[8,512]{1,0:T(8,128)S(1)} %fusion.40), channel_id=1, replica_groups=mesh['row'=16,'col'=32] {'row'}, use_global_device_ids=true, to_apply=%region_4.5 | all-reduce | flops 4096 | bytes 32768 | tf_op jit(solution)/shard_map/psum | solution.py:47
  415.3 45.4 %all_gather.21 = f32[8,16384]{1,0:T(8,128)S(1)} all-gather(f32[8,512]{1,0:T(8,128)S(1)} %psum.52), channel_id=1, replica_groups=mesh['row'=16,'col'=32] {'col'}, dimensions={1}, use_global_device_ids=true | all-gather | bytes 540672 | tf_op jit(solution)/shard_map/all_gather | solution.py:48
  460.8 1.6 bitcast_select_fusion.3
  462.3 0.2 convolution_add_fusion.3
  462.6 0.0 copy-start.4
  462.6 0.0 copy-start.5
  462.6 55.9 %psum.53 = f32[8,512]{1,0:T(8,128)S(1)} all-reduce(f32[8,512]{1,0:T(8,128)S(1)} %convolution_add_fusion.3), channel_id=1, replica_groups=mesh['row'=16,'col'=32] {'row'}, use_global_device_ids=true, to_apply=%region_5.6 | all-reduce | flops 4096 | bytes 32768 | tf_op jit(solution)/shard_map/psum | solution.py:47
  518.5 44.6 %all_gather.22 = f32[8,16384]{1,0:T(8,128)S(1)} all-gather(f32[8,512]{1,0:T(8,128)S(1)} %psum.53), channel_id=1, replica_groups=mesh['row'=16,'col'=32] {'col'}, dimensions={1}, use_global_device_ids=true | all-gather | bytes 540672 | tf_op jit(solution)/shard_map/all_gather | solution.py:48
  563.1 1.6 fusion.18
  564.6 0.2 convolution_add_fusion.2
  564.9 55.8 %psum.54 = f32[8,512]{1,0:T(8,128)S(1)} all-reduce(f32[8,512]{1,0:T(8,128)S(1)} %convolution_add_fusion.2), channel_id=1, replica_groups=mesh['row'=16,'col'=32] {'row'}, use_global_device_ids=true, to_apply=%region_6.7 | all-reduce | flops 4096 | bytes 32768 | tf_op jit(solution)/shard_map/psum | solution.py:47
  620.6 42.0 %all_gather.23 = f32[8,16384]{1,0:T(8,128)S(1)} all-gather(f32[8,512]{1,0:T(8,128)S(1)} %psum.54), channel_id=1, replica_groups=mesh['row'=16,'col'=32] {'col'}, dimensions={1}, use_global_device_ids=true | all-gather | bytes 540672 | tf_op jit(solution)/shard_map/all_gather | solution.py:48
  662.6 1.6 bitcast_select_fusion.1
  664.2 0.0 copy-start.3
  664.2 0.0 copy-done
  664.2 0.0 copy-done.4
  664.2 0.0 copy-done.5
  664.2 0.6 fusion.2
  664.8 99.5 %psum.55 = bf16[8,1024]{1,0:T(8,128)(2,1)S(1)} all-reduce(f32[8,1024]{1,0:T(8,128)S(1)} %fusion.2), channel_id=1, replica_groups=mesh['row'=16,'col'=32] {'row','col'}, use_global_device_ids=true, to_apply=%region_7.8 | all-reduce | flops 8192 | bytes 49152 | tf_op jit(solution)/shard_map/psum | solution.py:67
  764.4 0.4 fusion.7
  764.8 0.0 copy-done.3
  764.8 0.7 copy.11
  (2 shorter events, 0.0 us)
Async XLA Ops:
  0.6 663.6 %copy-start = (bf16[1024,1,1024]{2,0,1:T(8,128)(2,1)S(1)}, bf16[1024,1,1024]{2,0,1:T(8,128)(2,1)}, u32[]{:S(2)}) copy-start(bf16[1024,1,1024]{2,0,1:T(8,128)(2,1)} %param.13) | copy-start | bytes 6291460
  0.6 143.2 %copy-start.1 = (bf16[1024,512]{1,0:T(8,128)(2,1)S(1)}, bf16[1024,512]{1,0:T(8,128)(2,1)}, u32[]{:S(2)}) copy-start(bf16[1024,512]{1,0:T(8,128)(2,1)} %param.7) | copy-start | bytes 3145732
  0.7 123.3 %copy-start.2 = (f32[8,1024]{1,0:T(8,128)S(1)}, f32[8,1024]{1,0:T(8,128)}, u32[]{:S(2)}) copy-start(f32[8,1024]{1,0:T(8,128)} %param.9) | copy-start | bytes 98308
  462.6 201.6 %copy-start.4 = (f32[1,1024]{1,0:T(1,128)S(1)}, f32[1,1024]{1,0:T(1,128)}, u32[]{:S(2)}) copy-start(f32[1,1024]{1,0:T(1,128)} %param.11) | copy-start | bytes 12292
  462.6 201.6 %copy-start.5 = (f32[1,1024]{1,0:T(1,128)S(1)}, f32[1,1024]{1,0:T(1,128)}, u32[]{:S(2)}) copy-start(f32[1,1024]{1,0:T(1,128)} %param.12) | copy-start | bytes 12292
  664.2 100.6 %copy-start.3 = (f32[8,1024]{1,0:T(8,128)}, f32[8,1024]{1,0:T(8,128)S(1)}, u32[]{:S(2)}) copy-start(f32[8,1024]{1,0:T(8,128)S(1)} %get-tuple-element.23) | copy-start | bytes 98308
where the time goes:
time: 766 us; the launch traced here: 765 us
  blocking collectives  745 us (97%)
  matrix products  18.2 us (2%)
    psum x3, blocking collectives, on_device(): total_sum = lax.psum(pending, 'col')  289 us
    psum x3, blocking collectives, on_device(): column_sum = lax.psum(back_pending, 'row')  170 us
    all_gather x3, blocking collectives, on_device(): full_sum = lax.all_gather(column_sum, 'col', axis=1, tiled=True)  132 us
    psum x1, blocking collectives, on_device(): coords = lax.psum(partial_coords, ('row', 'col'))  99.5 us
    all_gather x3, blocking collectives, on_device(): whole = lax.all_gather(fresh, 'row', axis=1, tiled=True)  54.2 us

commit v1 on v0

--- a/solution.py
+++ b/solution.py
@@ -44,7 +44,11 @@
     back_out = jnp.zeros((vectors, rows_local), jnp.float32)
     for level in reversed(range(LEVELS)):
         if level < LEVELS - 1:
-            column_sum = lax.psum(back_pending, "row")
+            column_sum = back_pending
+            for hop in (1, 2, 4, 8):
+                column_sum = column_sum + lax.ppermute(
+                    column_sum, "row", [(dev, dev ^ hop) for dev in range(16)]
+                )
             full_sum = lax.all_gather(column_sum, "col", axis=1, tiled=True)
             here = lax.dynamic_slice_in_dim(full_sum, row_at * rows_local, rows_local, 1)
         else:

time: 766 us -> 629 us (0.82)
  blocking collectives: 745 us -> 548 us
  starting transfers between devices: 0 us -> 42.6 us
  waiting for transfers between devices: 0 us -> 20.5 us
    psum x3 -> x0, blocking collectives: 170 us -> none  [on_device(): column_sum = lax.psum(back_pending, 'row')]
    ppermute x0 -> x12, starting transfers between devices: none -> 42.6 us  [on_device(): lax.ppermute(column_sum, 'row', [(dev, dev ^ hop) for dev in range(16)])]
    all_gather x3, blocking collectives: 132 us -> 104 us  [on_device(): full_sum = lax.all_gather(column_sum, 'col', axis=1, tiled=True)]
    ppermute x0 -> x12, waiting for transfers between devices: none -> 20.5 us  [on_device(): lax.ppermute(column_sum, 'row', [(dev, dev ^ hop) for dev in range(16)])]
  transfers between devices with their start and end apart: 0 -> 12, of which waited for: 0 -> 12; matrix products, arithmetic and copies ran while one was open for 0% -> 0% of each run, Pallas kernels for 0% -> 0%
where the time goes in v1:
time: 629 us
  blocking collectives  548 us (87%)
  starting transfers between devices  42.6 us (7%)
  waiting for transfers between devices  20.5 us (3%)
  matrix products  15.2 us (2%)
    psum x3, blocking collectives, on_device(): total_sum = lax.psum(pending, 'col')  289 us
    all_gather x3, blocking collectives, on_device(): full_sum = lax.all_gather(column_sum, 'col', axis=1, tiled=True)  104 us
    psum x1, blocking collectives, on_device(): coords = lax.psum(partial_coords, ('row', 'col'))  100 us
    all_gather x3, blocking collectives, on_device(): whole = lax.all_gather(fresh, 'row', axis=1, tiled=True)  54.2 us
    ppermute x12, starting transfers between devices, on_device(): lax.ppermute(column_sum, 'row', [(dev, dev ^ hop) for dev in range(16)])  42.6 us
    ppermute x12, waiting for transfers between devices, on_device(): lax.ppermute(column_sum, 'row', [(dev, dev ^ hop) for dev in range(16)])  20.5 us
  transfers between devices with their start and end apart: 12, of which 12 were waited for; matrix products, arithmetic and copies ran while one was open for 0% of the time, Pallas kernels for 0%

profile of v1, /device:TPU:1, one launch (start us, length us, event | category | flops | bytes accessed | tf_op | source)
XLA Modules:
  0.0 628.5 jit_solution(14016891329895526743)
XLA Ops:
  0.6 0.0 copy-start
  0.6 0.0 copy-start.3
  0.7 0.0 copy-start.1
  0.7 0.9 select_reduce_fusion
  1.6 0.1 broadcast_bitcast_fusion
  1.7 2.0 select_convert_fusion.5
  3.7 19.7 %all_gather.18 = bf16[8,16384]{1,0:T(8,128)(2,1)S(1)} all-gather(bf16[8,1024]{1,0:T(8,128)(2,1)S(1)} %get-tuple-element.14), channel_id=1, replica_groups=mesh['row'=16,'col'=32] {'row'}, dimensions={1}, use_global_device_ids=true | all-gather | bytes 278528 | tf_op jit(solution)/shard_map/all_gather | solution.py:40
  23.3 1.6 fusion.64
  24.9 99.0 %psum.28 = f32[8,1024]{1,0:T(8,128)S(1)} all-reduce(f32[8,1024]{1,0:T(8,128)S(1)} %fusion.64), channel_id=1, replica_groups=mesh['row'=16,'col'=32] {'col'}, use_global_device_ids=true, to_apply=%region_1.2 | all-reduce | flops 8192 | bytes 65536 | tf_op jit(solution)/shard_map/psum | solution.py:29
  123.9 0.0 copy-done.3
  123.9 2.0 select_convert_fusion.4
  125.9 17.9 %all_gather.19 = bf16[8,16384]{1,0:T(8,128)(2,1)S(1)} all-gather(bf16[8,1024]{1,0:T(8,128)(2,1)S(1)} %get-tuple-element.8), channel_id=1, replica_groups=mesh['row'=16,'col'=32] {'row'}, dimensions={1}, use_global_device_ids=true | all-gather | bytes 278528 | tf_op jit(solution)/shard_map/all_gather | solution.py:40
  143.8 0.0 copy-done.1
  143.8 0.4 convolution_add_fusion.1
  144.2 95.2 %psum.29 = f32[8,1024]{1,0:T(8,128)S(1)} all-reduce(f32[8,1024]{1,0:T(8,128)S(1)} %convolution_add_fusion.1), channel_id=1, replica_groups=mesh['row'=16,'col'=32] {'col'}, use_global_device_ids=true, to_apply=%region_2.3 | all-reduce | flops 8192 | bytes 65536 | tf_op jit(solution)/shard_map/psum | solution.py:29
  239.4 2.0 select_convert_fusion.3
  241.4 16.6 %all_gather.20 = bf16[8,16384]{1,0:T(8,128)(2,1)S(1)} all-gather(bf16[8,1024]{1,0:T(8,128)(2,1)S(1)} %get-tuple-element.17), channel_id=1, replica_groups=mesh['row'=16,'col'=32] {'row'}, dimensions={1}, use_global_device_ids=true | all-gather | bytes 278528 | tf_op jit(solution)/shard_map/all_gather | solution.py:40
  258.0 0.4 convolution_add_fusion
  258.4 94.9 %psum.30 = f32[8,1024]{1,0:T(8,128)S(1)} all-reduce(f32[8,1024]{1,0:T(8,128)S(1)} %convolution_add_fusion), channel_id=1, replica_groups=mesh['row'=16,'col'=32] {'col'}, use_global_device_ids=true, to_apply=%region_3.4 | all-reduce | flops 8192 | bytes 65536 | tf_op jit(solution)/shard_map/psum | solution.py:29
  353.3 0.0 copy-start.2
  353.3 2.0 bitcast_select_fusion.5
  355.4 1.6 fusion.22
  357.0 0.2 fusion.40
  357.2 2.8 collective-permute-start
  360.0 1.6 collective-permute-done
  361.7 4.2 collective-permute-start.1
  365.9 1.8 collective-permute-done.1
  367.7 2.8 collective-permute-start.2
  370.5 2.0 collective-permute-done.2
  372.5 4.2 collective-permute-start.3
  376.7 1.7 collective-permute-done.3
  378.5 35.8 %all_gather.21 = f32[8,16384]{1,0:T(8,128)S(1)} all-gather(f32[8,512]{1,0:T(8,128)S(1)} %add.75), channel_id=1, replica_groups=mesh['row'=16,'col'=32] {'col'}, dimensions={1}, use_global_device_ids=true | all-gather | bytes 540672 | tf_op jit(solution)/shard_map/all_gather | solution.py:52
  414.3 0.0 copy-done.2
  414.3 0.5 bitcast_select_fusion.3
  414.8 0.2 convolution_add_fusion.3
  415.1 3.0 collective-permute-start.4
  418.0 1.6 collective-permute-done.4
  419.7 4.2 collective-permute-start.5
  423.9 1.8 collective-permute-done.5
  425.7 2.9 collective-permute-start.6
  428.6 1.5 collective-permute-done.6
  430.2 4.3 collective-permute-start.7
  434.4 1.7 collective-permute-done.7
  436.1 35.4 %all_gather.22 = f32[8,16384]{1,0:T(8,128)S(1)} all-gather(f32[8,512]{1,0:T(8,128)S(1)} %add.80), channel_id=1, replica_groups=mesh['row'=16,'col'=32] {'col'}, dimensions={1}, use_global_device_ids=true | all-gather | bytes 540672 | tf_op jit(solution)/shard_map/all_gather | solution.py:52
  471.6 0.5 fusion.18
  472.1 0.2 convolution_add_fusion.2
  472.3 2.8 collective-permute-start.8
  475.2 1.6 collective-permute-done.8
  476.8 4.2 collective-permute-start.9
  481.0 1.8 collective-permute-done.9
  482.8 2.9 collective-permute-start.10
  485.7 1.5 collective-permute-done.10
  487.3 4.3 collective-permute-start.11
  491.6 1.7 collective-permute-done.11
  493.3 32.8 %all_gather.23 = f32[8,16384]{1,0:T(8,128)S(1)} all-gather(f32[8,512]{1,0:T(8,128)S(1)} %add.85), channel_id=1, replica_groups=mesh['row'=16,'col'=32] {'col'}, dimensions={1}, use_global_device_ids=true | all-gather | bytes 540672 | tf_op jit(solution)/shard_map/all_gather | solution.py:52
  526.1 0.5 bitcast_select_fusion.1
  526.6 0.0 copy-done
  526.6 0.0 copy-done.5
  526.6 0.0 copy-done.6
  526.6 0.6 fusion.2
  527.3 100.2 %psum.31 = bf16[8,1024]{1,0:T(8,128)(2,1)S(1)} all-reduce(f32[8,1024]{1,0:T(8,128)S(1)} %fusion.2), channel_id=1, replica_groups=mesh['row'=16,'col'=32] {'row','col'}, use_global_device_ids=true, to_apply=%region_4.5 | all-reduce | flops 8192 | bytes 49152 | tf_op jit(solution)/shard_map/psum | solution.py:71
  627.5 0.4 fusion.7
  627.9 0.0 copy-done.4
  627.9 0.7 copy.11
  (17 shorter events, 0.1 us)
Async XLA Ops:
  0.6 526.0 %copy-start = (bf16[1024,1,1024]{2,0,1:T(8,128)(2,1)S(1)}, bf16[1024,1,1024]{2,0,1:T(8,128)(2,1)}, u32[]{:S(2)}) copy-start(bf16[1024,1,1024]{2,0,1:T(8,128)(2,1)} %param.13) | copy-start | bytes 6291460
  0.6 123.3 %copy-start.3 = (f32[8,1024]{1,0:T(8,128)S(1)}, f32[8,1024]{1,0:T(8,128)}, u32[]{:S(2)}) copy-start(f32[8,1024]{1,0:T(8,128)} %param.9) | copy-start | bytes 98308
  0.7 143.2 %copy-start.1 = (bf16[1024,512]{1,0:T(8,128)(2,1)S(1)}, bf16[1024,512]{1,0:T(8,128)(2,1)}, u32[]{:S(2)}) copy-start(bf16[1024,512]{1,0:T(8,128)(2,1)} %param.7) | copy-start | bytes 3145732
  353.3 61.0 %copy-start.2 = (f32[8,128,128]{2,1,0:T(8,128)S(1)}, f32[8,128,128]{2,1,0:T(8,128)}, u32[]{:S(2)}) copy-start(f32[8,128,128]{2,1,0:T(8,128)} %param.8) | copy-start | bytes 1572868
  357.2 4.5 collective-permute-start
  361.7 6.0 collective-permute-start.1
  367.7 4.8 collective-permute-start.2
  372.5 6.0 collective-permute-start.3
  415.1 111.5 %copy-start.5 = (f32[1,1024]{1,0:T(1,128)S(1)}, f32[1,1024]{1,0:T(1,128)}, u32[]{:S(2)}) copy-start(f32[1,1024]{1,0:T(1,128)} %param.11) | copy-start | bytes 12292
  415.1 111.5 %copy-start.6 = (f32[1,1024]{1,0:T(1,128)S(1)}, f32[1,1024]{1,0:T(1,128)}, u32[]{:S(2)}) copy-start(f32[1,1024]{1,0:T(1,128)} %param.12) | copy-start | bytes 12292
  415.1 4.6 collective-permute-start.4
  419.7 6.0 collective-permute-start.5
  425.7 4.5 collective-permute-start.6
  430.2 6.0 collective-permute-start.7
  472.3 4.5 collective-permute-start.8
  476.8 6.0 collective-permute-start.9
  482.8 4.5 collective-permute-start.10
  487.3 6.0 collective-permute-start.11
  526.6 101.3 %copy-start.4 = (f32[8,1024]{1,0:T(8,128)}, f32[8,1024]{1,0:T(8,128)S(1)}, u32[]{:S(2)}) copy-start(f32[8,1024]{1,0:T(8,128)S(1)} %get-tuple-element.23) | copy-start | bytes 98308
